TPU v7x, 128 devices: a whole 4x4x4 slice. The times are simulated.
128 devices in a mesh: row: 16 (over x, z_hi, core), col: 8 (over z_lo, y).
Axes of the slice: x: 4, y: 4, z: 4 (z_hi: 2, z_lo: 2; z = z_hi * 2 + z_lo), core: 2. Of those that a mesh axis runs over, the one named last changes fastest.
Arguments:
- vectors: bfloat16 [16, 262144], P(None, ('row', 'col'))
- stiffness: bfloat16 [16, 8, 192, 128, 128], P('row', 'col'), may hold values from -0.109375 to 0.109375
- block_row: int32 [16, 8, 192], P('row', 'col'), may hold values from 0 to 127
- block_col: int32 [16, 8, 192], P('row', 'col'), may hold values from 0 to 255
- block_count: int32 [16, 8], P('row', 'col'), may hold values from 1 to 192, as said below
- diag_blocks: bfloat16 [2048, 128, 128], P(('row', 'col'))
- precond: bfloat16 [2048, 128, 128], P(('row', 'col')), may hold values from -0.5 to 0.5
Outputs:
- image: float32 [16, 262144], P(None, ('row', 'col'))
- search: bfloat16 [16, 262144], P(None, ('row', 'col'))
Inputs may be any that keep to these rules, and one draw needn't show every extreme that they name: block_count is at most 192 and equals 192 on at least one grid cell in every draw.
All inputs are finite; a program needn't handle non-finite values.
Results may differ from a plain program's by a relative error of at most 0.0051.
Values may be sent and summed in bfloat16 or wider, within the bound.
No kernel may reach another device: no remote copies, remote signals or barrier semaphores. Data moves between devices by JAX's collectives and lax.ppermute only.
A program may use at most 128 MiB of HBM per device.

v0:
```python
import jax
import jax.numpy as jnp
from jax import lax
from jax.sharding import PartitionSpec as P


def per_device(vectors, stiffness, block_row, block_col, block_count, diag_blocks, precond):
    blocks = stiffness[0, 0]
    rows_index = block_row[0, 0]
    cols_index = block_col[0, 0]
    live_count = block_count[0, 0]
    vec_count = vectors.shape[0]
    owned = diag_blocks.shape[0]
    block_len = diag_blocks.shape[1]
    slots = blocks.shape[0]
    row_devs = lax.axis_size("row")
    col_devs = lax.axis_size("col")
    vectors_f = vectors.astype(jnp.float32)
    lengths_local = jnp.sum(vectors_f * vectors_f, axis=1)
    everything = lax.all_gather(vectors, ("row", "col"), axis=1, tiled=True)
    spread = everything.reshape(vec_count, row_devs, col_devs, owned, block_len)
    row_part = lax.dynamic_index_in_dim(spread, lax.axis_index("row"), 1, False)
    col_part = lax.dynamic_index_in_dim(spread, lax.axis_index("col"), 2, False)
    row_part = row_part.reshape(vec_count, col_devs * owned, block_len)
    col_part = col_part.reshape(vec_count, row_devs * owned, block_len)
    picked_col = jnp.take(col_part, cols_index, axis=1)
    picked_row = jnp.take(row_part, rows_index, axis=1)
    toward_row = jnp.einsum("knb,nab->kna", picked_col, blocks, preferred_element_type=jnp.float32)
    toward_col = jnp.einsum("kna,nab->knb", picked_row, blocks, preferred_element_type=jnp.float32)
    live = jnp.arange(slots, dtype=jnp.int32) < live_count
    row_onehot = (
        (rows_index[None, :] == jnp.arange(col_devs * owned, dtype=jnp.int32)[:, None])
        & live[None, :]
    ).astype(jnp.float32)
    col_onehot = (
        (cols_index[None, :] == jnp.arange(row_devs * owned, dtype=jnp.int32)[:, None])
        & live[None, :]
    ).astype(jnp.float32)
    row_partial = jnp.einsum(
        "kna,gn->kga",
        toward_row,
        row_onehot,
        precision=lax.Precision.HIGHEST,
        preferred_element_type=jnp.float32,
    )
    col_partial = jnp.einsum(
        "kna,gn->kga",
        toward_col,
        col_onehot,
        precision=lax.Precision.HIGHEST,
        preferred_element_type=jnp.float32,
    )
    zero_term = jnp.zeros((vec_count, row_devs, col_devs, owned * block_len), jnp.float32)
    term = lax.dynamic_update_index_in_dim(
        zero_term,
        row_partial.reshape(vec_count, col_devs, owned * block_len),
        lax.axis_index("row"),
        1,
    )
    term = term + lax.dynamic_update_index_in_dim(
        zero_term,
        col_partial.reshape(vec_count, row_devs, owned * block_len),
        lax.axis_index("col"),
        2,
    )
    mine = lax.psum_scatter(
        term.reshape(vec_count, row_devs * col_devs * owned * block_len),
        ("row", "col"),
        scatter_dimension=1,
        tiled=True,
    )
    own_vec = vectors.reshape(vec_count, owned, block_len)
    diag_term = jnp.einsum("nab,knb->kna", diag_blocks, own_vec, preferred_element_type=jnp.float32)
    diag_term = diag_term + jnp.einsum(
        "nba,knb->kna", diag_blocks, own_vec, preferred_element_type=jnp.float32
    )
    image = mine + diag_term.reshape(vec_count, owned * block_len)
    inner_local = jnp.sum(vectors_f * image, axis=1)
    lengths, inner = lax.psum((lengths_local, inner_local), ("row", "col"))
    theta = inner / lengths
    resid = (image - theta[:, None] * vectors_f).astype(jnp.bfloat16)
    search = jnp.einsum(
        "nab,knb->kna",
        precond,
        resid.reshape(vec_count, owned, block_len),
        preferred_element_type=jnp.float32,
    )
    return (image, search.reshape(vec_count, owned * block_len).astype(jnp.bfloat16))


def solution(mesh):
    placed = (
        P(None, ("row", "col")),
        P("row", "col", None, None, None),
        P("row", "col", None),
        P("row", "col", None),
        P("row", "col"),
        P(("row", "col"), None, None),
        P(("row", "col"), None, None),
    )
    return jax.shard_map(
        per_device,
        mesh=mesh,
        in_specs=placed,
        out_specs=(P(None, ("row", "col")), P(None, ("row", "col"))),
        check_vma=False,
    )
```

profile of v0, /device:TPU:1, one launch (start us, length us, event | category | flops | bytes accessed | tf_op | source)
XLA Modules:
  0.0 1170.2 jit_solution(11257969639220290386)
XLA Ops:
  7.2 0.0 copy-start
  7.2 0.0 all-gather.2.cloned.1.call-start
  7.2 0.7 all-gather.2.cloned.1.call-update
  7.9 0.0 reduce-scatter.2.cloned.1.call-start
  8.6 0.7 compare_select_fusion
  9.4 0.7 compare_and_fusion
  10.1 315.9 %all-gather.2.cloned.1.call-done = bf16[16,262144]{1,0:T(8,128)(2,1)} async-done(((bf16[16,2048]{1,0:T(8,128)(2,1)}), bf16[16,262144]{1,0:T(8,128)(2,1)}) %all-gather.2.cloned.1.call-update) | async-done | bytes 8388624 | tf_op jit(solution)/shard_map/all_gather | solution.py:20
  325.9 8.1 copy.31
  334.0 1.1 constant_dynamic-slice_fusion
  335.1 1.5 constant_dynamic-slice_fusion.1
  336.6 0.0 copy-start.4
  336.6 1.7 copy.25
  338.3 0.3 copy.26
  338.7 0.8 gather_fusion.1
  339.4 4.1 fusion
  343.5 0.0 copy-done.4
  343.5 2.9 convolution_bitcast_fusion
  346.5 0.0 copy-start.5
  346.5 1.7 broadcast_in_dim.39
  348.2 2.0 gather_fusion
  350.2 5.5 fusion.2
  355.7 0.0 copy-done.5
  355.7 2.3 fusion.9
  358.0 2.3 broadcast_in_dim.37
  360.3 3.3 copy.15
  363.6 7.9 broadcast_in_dim.34
  371.4 20.5 %dynamic_update_slice.10 = f32[16,16,8,2048]{3,1,0,2:T(8,128)} dynamic-update-slice(f32[16,16,8,2048]{3,1,0,2:T(8,128)} %broadcast_in_dim.34, f32[16,1,8,2048]{3,1,0,2:T(1,128)} %copy.15, s32[]{:T(128)} %constant.42.clone.1, s32[]{:T(128)S(6)} %select_n.55, s32[]{:T(128)} %constant.42.clone.1, s32[]{:T(128)} %constant.42.clone.1) | dynamic-update-slice | bytes 2097156 | tf_op jit(solution)/shard_map/jit(dynamic_update_index_in_dim)/dynamic_update_slice | solution.py:54
  391.9 3.3 add_dynamic-update-slice_fusion
  395.2 15.5 %copy.17 = f32[16,16,8,2048]{3,2,1,0:T(8,128)S(1)} copy(f32[16,16,8,2048]{3,1,0,2:T(8,128)} %add_dynamic-update-slice_fusion) | data formatting | bytes 33554432 | tf_op jit(solution)/shard_map/add | solution.py:60
  410.7 20.1 %copy.32 = f32[2,8,128,2048]{3,1,2,0:T(8,128)} copy(f32[2,8,128,2048]{3,2,1,0:T(8,128)S(1)} %bitcast.82) | data formatting | bytes 33554432
  430.8 0.0 copy-start.1
  430.8 0.0 copy-start.2
  430.8 0.0 reduce-scatter.2.cloned.1.call-update
  430.8 0.0 copy-done
  430.8 0.8 copy-done.1
  431.6 0.4 fusion.38
  432.0 0.3 fusion.12
  432.2 650.6 %reduce-scatter.2.cloned.1.call-done = f32[16,2048]{1,0:T(8,128)} async-done(((f32[16,262144]{1,0:T(8,128)}), f32[16,2048]{1,0:T(8,128)}) %reduce-scatter.2.cloned.1.call-update) | async-done | bytes 131088 | tf_op jit(solution)/shard_map/reduce_scatter | solution.py:66
  1082.9 1.0 fusion.26
  1083.9 0.0 copy-start.3
  1083.9 78.4 %all-reduce = (f32[16]{0:T(128)S(1)}, f32[16]{0:T(128)S(1)}) all-reduce(f32[16]{0:T(128)S(1)} %get-tuple-element.3, f32[16]{0:T(128)S(1)} %get-tuple-element.2), channel_id=1, replica_groups=mesh['row'=16,'col'=8] {'row','col'}, use_global_device_ids=true, to_apply=%region_2.3 | all-reduce | flops 32 | bytes 256 | tf_op jit(solution)/shard_map/psum | solution.py:79
  1162.3 0.0 copy-done.2
  1162.3 0.4 fusion.13
  1162.7 0.7 copy.58
  1163.4 0.0 copy-done.3
  (4 shorter events, 0.0 us)
Async XLA Ops:
  7.2 423.6 %copy-start = (bf16[16,128,128]{2,1,0:T(8,128)(2,1)S(1)}, bf16[16,128,128]{2,1,0:T(8,128)(2,1)}, u32[]{:S(2)}) copy-start(bf16[16,128,128]{2,1,0:T(8,128)(2,1)} %param.12) | copy-start | bytes 1572868
  7.2 318.8 %all-gather.2.cloned.1.call-start = ((), (), s32[]{:S(2)}) async-start(), calls=%async_computation.1 | async-start | bytes 8454144 | tf_op jit(solution)/shard_map/all_gather | solution.py:20
  7.9 1075.0 %reduce-scatter.2.cloned.1.call-start = ((), (), s32[]{:S(2)}) async-start(), calls=%async_computation.2 | async-start | bytes 16908288 | tf_op jit(solution)/shard_map/reduce_scatter | solution.py:66
  336.6 6.9 copy-start.4
  346.5 9.2 copy-start.5
  430.8 0.8 copy-start.1
  430.8 731.5 %copy-start.2 = (bf16[16,128,128]{2,1,0:T(8,128)(2,1)S(1)}, bf16[16,128,128]{2,1,0:T(8,128)(2,1)}, u32[]{:S(2)}) copy-start(bf16[16,128,128]{2,1,0:T(8,128)(2,1)} %param.13) | copy-start | bytes 1572868
  1083.9 79.5 %copy-start.3 = (f32[16,2048]{1,0:T(8,128)}, f32[16,2048]{1,0:T(8,128)S(1)}, u32[]{:S(2)}) copy-start(f32[16,2048]{1,0:T(8,128)S(1)} %get-tuple-element.6) | copy-start | bytes 393220
Sparse Core Ops, SparseCore 0:
  9.7 316.1 all-gather.1
  430.9 651.9 reduce-scatter.1
where the time goes:
time: 1170 us
  waiting for transfers between devices  967 us (83%)
  local copies, waits for them, and re-layouts  88.2 us (8%)
  blocking collectives  78.4 us (7%)
  matrix products  15.8 us (1%)
  between operations  14.8 us (1%)
    reduce_scatter x1, waiting for transfers between devices, per_device(): lax.psum_scatter(term.reshape(vec_count, row_devs * col_devs * owned * bl...  651 us
    all_gather x1, waiting for transfers between devices, per_device(): everything = lax.all_gather(vectors, ('row', 'col'), axis=1, tiled=True)  316 us
    psum x1, blocking collectives, per_device(): lengths, inner = lax.psum((lengths_local, inner_local), ('row', 'col'))  78.4 us
    unnamed x16, local copies, waits for them, and re-layouts  31 us
  transfers between devices with their start and end apart: 2, of which 2 were waited for; matrix products, arithmetic and copies ran while one was open for 0% of the time, Pallas kernels for 0%

commit v1 on v0

--- a/solution.py
+++ b/solution.py
@@ -2,6 +2,7 @@
 import jax.numpy as jnp
 from jax import lax
 from jax.sharding import PartitionSpec as P
+from jax.lax import all_to_all, axis_size
 
 
 def per_device(vectors, stiffness, block_row, block_col, block_count, diag_blocks, precond):
@@ -17,7 +18,15 @@
     col_devs = lax.axis_size("col")
     vectors_f = vectors.astype(jnp.float32)
     lengths_local = jnp.sum(vectors_f * vectors_f, axis=1)
-    everything = lax.all_gather(vectors, ("row", "col"), axis=1, tiled=True)
+    everything = jnp.concatenate(
+        all_to_all(
+            jnp.stack([vectors for _ in range(axis_size(("row", "col")))], axis=0),
+            ("row", "col"),
+            0,
+            0,
+        ),
+        axis=1,
+    )
     spread = everything.reshape(vec_count, row_devs, col_devs, owned, block_len)
     row_part = lax.dynamic_index_in_dim(spread, lax.axis_index("row"), 1, False)
     col_part = lax.dynamic_index_in_dim(spread, lax.axis_index("col"), 2, False)

time: 1170 us -> 981 us (0.84)
  waiting for transfers between devices: 967 us -> 760 us
  starting transfers between devices: 0.08 us -> 12 us
    all_gather x1 -> x0, waiting for transfers between devices: 316 us -> none  [per_device(): everything = lax.all_gather(vectors, ('row', 'col'), axis=1, tiled=True)]
    all_to_all x0 -> x1, waiting for transfers between devices: none -> 105 us  [per_device(): all_to_all(jnp.stack([vectors for _ in range(axis_size(('row', 'col')))],...]
    all_to_all x0 -> x1, starting transfers between devices: none -> 12 us  [per_device(): all_to_all(jnp.stack([vectors for _ in range(axis_size(('row', 'col')))],...]
where the time goes in v1:
time: 981 us; the launch traced here: 980 us
  waiting for transfers between devices  760 us (77%)
  local copies, waits for them, and re-layouts  95.2 us (10%)
  blocking collectives  78.3 us (8%)
  matrix products  15.8 us (2%)
  between operations  14.8 us (2%)
  starting transfers between devices  12 us (1%)
    reduce_scatter x1, waiting for transfers between devices, per_device(): lax.psum_scatter(term.reshape(vec_count, row_devs * col_devs * owned * bl...  655 us
    all_to_all x1, waiting for transfers between devices, per_device(): all_to_all(jnp.stack([vectors for _ in range(axis_size(('row', 'col')))],...  105 us
    psum x1, blocking collectives, per_device(): lengths, inner = lax.psum((lengths_local, inner_local), ('row', 'col'))  78.3 us
    unnamed x16, local copies, waits for them, and re-layouts  31 us
    dynamic_update_slice x1, local copies, waits for them, and re-layouts, per_device(): lax.dynamic_update_index_in_dim(zero_term, row_partial.reshape(vec_count,...  20.4 us
  transfers between devices with their start and end apart: 2, of which 2 were waited for; matrix products, arithmetic and copies ran while one was open for 0% of the time, Pallas kernels for 0%

profile of v1, /device:TPU:1, one launch (start us, length us, event | category | flops | bytes accessed | tf_op | source)
XLA Modules:
  0.0 980.3 jit_solution(263160014986501577)
XLA Ops:
  7.2 0.0 copy-start
  7.2 5.2 stack.2
  12.4 0.0 copy-start.4
  12.4 0.0 copy-start.5
  12.4 12.0 %all-to-all-start = ((bf16[128,16,2048]{2,1,0:T(8,128)(2,1)}), bf16[128,16,2048]{2,1,0:T(8,128)(2,1)}, u32[]{:S(2)}, u32[]{:S(2)}) async-start(bf16[128,16,2048]{2,1,0:T(8,128)(2,1)} %stack.2), calls=%async_computation | async-start | bytes 16777216 | tf_op jit(solution)/shard_map/all_to_all | solution.py:22
  24.3 0.0 reduce-scatter.2.cloned.1.call-start
  25.0 0.0 copy-done.4
  25.1 0.0 copy-done.5
  25.1 105.2 %all-to-all-done = bf16[128,16,2048]{2,1,0:T(8,128)(2,1)} async-done(((bf16[128,16,2048]{2,1,0:T(8,128)(2,1)}), bf16[128,16,2048]{2,1,0:T(8,128)(2,1)}, u32[]{:S(2)}, u32[]{:S(2)}) %all-to-all-start) | async-done | bytes 8388640 | tf_op jit(solution)/shard_map/all_to_all | solution.py:22
  130.4 9.8 copy.54
  140.1 1.1 constant_dynamic-slice_fusion
  141.2 1.4 constant_dynamic-slice_fusion.1
  142.6 0.3 copy.48
  142.9 1.7 copy.36
  144.6 0.3 copy.39
  145.0 0.8 gather_fusion.1
  145.8 4.1 fusion.10
  149.9 2.9 convolution_bitcast_fusion
  152.8 1.7 broadcast_in_dim.39
  154.5 2.0 gather_fusion
  156.5 5.5 fusion.7
  162.0 2.3 fusion.13
  164.3 2.4 broadcast_in_dim.37
  166.6 3.3 copy.38
  169.9 7.9 broadcast_in_dim.34
  177.8 20.4 %dynamic_update_slice.10 = f32[16,16,8,2048]{3,1,0,2:T(8,128)} dynamic-update-slice(f32[16,16,8,2048]{3,1,0,2:T(8,128)} %broadcast_in_dim.34, f32[16,1,8,2048]{3,1,0,2:T(1,128)} %copy.38, s32[]{:T(128)} %constant.42.clone.1, s32[]{:T(128)S(6)} %select_n.55, s32[]{:T(128)} %constant.42.clone.1, s32[]{:T(128)} %constant.42.clone.1) | dynamic-update-slice | bytes 2097156 | tf_op jit(solution)/shard_map/jit(dynamic_update_index_in_dim)/dynamic_update_slice | solution.py:63
  198.1 3.2 add_dynamic-update-slice_fusion
  201.3 15.5 %copy.41 = f32[16,16,8,2048]{3,2,1,0:T(8,128)S(1)} copy(f32[16,16,8,2048]{3,1,0,2:T(8,128)} %add_dynamic-update-slice_fusion) | data formatting | bytes 33554432 | tf_op jit(solution)/shard_map/add | solution.py:69
  216.8 20.1 %copy.55 = f32[2,8,128,2048]{3,1,2,0:T(8,128)} copy(f32[2,8,128,2048]{3,2,1,0:T(8,128)S(1)} %bitcast.86) | data formatting | bytes 33554432
  236.9 0.0 copy-start.1
  236.9 0.0 copy-start.2
  236.9 0.0 reduce-scatter.2.cloned.1.call-update
  236.9 0.0 copy-done
  236.9 0.8 copy-done.1
  237.7 0.4 fusion.42
  238.1 0.3 fusion.16
  238.4 654.7 %reduce-scatter.2.cloned.1.call-done = f32[16,2048]{1,0:T(8,128)} async-done(((f32[16,262144]{1,0:T(8,128)}), f32[16,2048]{1,0:T(8,128)}) %reduce-scatter.2.cloned.1.call-update) | async-done | bytes 131088 | tf_op jit(solution)/shard_map/reduce_scatter | solution.py:75
  893.1 1.0 fusion.30
  894.2 0.0 copy-start.3
  894.2 78.3 %all-reduce = (f32[16]{0:T(128)S(1)}, f32[16]{0:T(128)S(1)}) all-reduce(f32[16]{0:T(128)S(1)} %get-tuple-element.3, f32[16]{0:T(128)S(1)} %get-tuple-element.2), channel_id=1, replica_groups=mesh['row'=16,'col'=8] {'row','col'}, use_global_device_ids=true, to_apply=%region_2.3 | all-reduce | flops 32 | bytes 256 | tf_op jit(solution)/shard_map/psum | solution.py:88
  972.4 0.0 copy-done.2
  972.4 0.4 fusion.17
  972.8 0.7 copy.77
  973.5 0.0 copy-done.3
  (7 shorter events, 0.1 us)
Async XLA Ops:
  7.2 229.8 %copy-start = (bf16[16,128,128]{2,1,0:T(8,128)(2,1)S(1)}, bf16[16,128,128]{2,1,0:T(8,128)(2,1)}, u32[]{:S(2)}) copy-start(bf16[16,128,128]{2,1,0:T(8,128)(2,1)} %param.12) | copy-start | bytes 1572868
  12.4 12.7 %copy-start.4 = (s32[1,1,192]{2,1,0:T(1,128)S(1)}, s32[1,1,192]{2,1,0:T(1,128)}, u32[]{:S(2)}) copy-start(s32[1,1,192]{2,1,0:T(1,128)} %param.10) | copy-start | bytes 2308
  12.4 12.7 %copy-start.5 = (s32[1,1,192]{2,1,0:T(1,128)S(1)}, s32[1,1,192]{2,1,0:T(1,128)}, u32[]{:S(2)}) copy-start(s32[1,1,192]{2,1,0:T(1,128)} %param.9) | copy-start | bytes 2308
  12.4 118.0 %all-to-all-start = ((bf16[128,16,2048]{2,1,0:T(8,128)(2,1)}), bf16[128,16,2048]{2,1,0:T(8,128)(2,1)}, u32[]{:S(2)}, u32[]{:S(2)}) async-start(bf16[128,16,2048]{2,1,0:T(8,128)(2,1)} %stack.2), calls=%async_computation | async-start | bytes 16777216 | tf_op jit(solution)/shard_map/all_to_all | solution.py:22
  24.3 868.8 %reduce-scatter.2.cloned.1.call-start = ((), (), s32[]{:S(2)}) async-start(), calls=%async_computation.2 | async-start | bytes 16908288 | tf_op jit(solution)/shard_map/reduce_scatter | solution.py:75
  236.9 0.8 copy-start.1
  236.9 735.5 %copy-start.2 = (bf16[16,128,128]{2,1,0:T(8,128)(2,1)S(1)}, bf16[16,128,128]{2,1,0:T(8,128)(2,1)}, u32[]{:S(2)}) copy-start(bf16[16,128,128]{2,1,0:T(8,128)(2,1)} %param.13) | copy-start | bytes 1572868
  894.2 79.3 %copy-start.3 = (f32[16,2048]{1,0:T(8,128)}, f32[16,2048]{1,0:T(8,128)S(1)}, u32[]{:S(2)}) copy-start(f32[16,2048]{1,0:T(8,128)S(1)} %get-tuple-element.6) | copy-start | bytes 393220
Sparse Core Ops, SparseCore 0:
  237.1 656.0 reduce-scatter.1

commit v2 on v0

--- a/solution.py
+++ b/solution.py
@@ -76,7 +76,12 @@
     )
     image = mine + diag_term.reshape(vec_count, owned * block_len)
     inner_local = jnp.sum(vectors_f * image, axis=1)
-    lengths, inner = lax.psum((lengths_local, inner_local), ("row", "col"))
+
+    def words_answer(m):
+        a_now = jax.lax.psum(m, axis_name="col")
+        return jax.lax.psum(a_now, axis_name="row")
+
+    lengths, inner = words_answer((lengths_local, inner_local))
     theta = inner / lengths
     resid = (image - theta[:, None] * vectors_f).astype(jnp.bfloat16)
     search = jnp.einsum(

time: 1170 us -> 1160 us (level)
  blocking collectives: 78.4 us -> 65.2 us
    psum x1 -> x2, blocking collectives: 78.4 us -> 65.2 us  [the longest x1 52.3 us: words_answer(): return jax.lax.psum(a_now, axis_name='row')]
where the time goes in v2:
time: 1160 us
  waiting for transfers between devices  966 us (83%)
  local copies, waits for them, and re-layouts  88.3 us (8%)
  blocking collectives  65.2 us (6%)
  matrix products  15.8 us (1%)
  between operations  14.8 us (1%)
    reduce_scatter x1, waiting for transfers between devices, per_device(): lax.psum_scatter(term.reshape(vec_count, row_devs * col_devs * owned * bl...  650 us
    all_gather x1, waiting for transfers between devices, per_device(): everything = lax.all_gather(vectors, ('row', 'col'), axis=1, tiled=True)  316 us
    psum x1, blocking collectives, words_answer(): return jax.lax.psum(a_now, axis_name='row')  52.3 us
    unnamed x16, local copies, waits for them, and re-layouts  31.1 us
  transfers between devices with their start and end apart: 2, of which 2 were waited for; matrix products, arithmetic and copies ran while one was open for 0% of the time, Pallas kernels for 0%

profile of v2, /device:TPU:1, one launch (start us, length us, event | category | flops | bytes accessed | tf_op | source)
XLA Modules:
  0.0 1156.3 jit_solution(209605455334010635)
XLA Ops:
  7.2 0.0 copy-start
  7.2 0.0 all-gather.2.cloned.1.call-start
  7.2 0.7 all-gather.2.cloned.1.call-update
  7.9 0.0 reduce-scatter.2.cloned.1.call-start
  8.6 0.7 compare_select_fusion
  9.4 0.7 compare_and_fusion
  10.1 315.9 %all-gather.2.cloned.1.call-done = bf16[16,262144]{1,0:T(8,128)(2,1)} async-done(((bf16[16,2048]{1,0:T(8,128)(2,1)}), bf16[16,262144]{1,0:T(8,128)(2,1)}) %all-gather.2.cloned.1.call-update) | async-done | bytes 8388624 | tf_op jit(solution)/shard_map/all_gather | solution.py:20
  325.9 8.1 copy.31
  334.0 1.1 constant_dynamic-slice_fusion
  335.1 1.5 constant_dynamic-slice_fusion.1
  336.6 0.0 copy-start.4
  336.6 1.7 copy.25
  338.3 0.3 copy.26
  338.6 0.8 gather_fusion.1
  339.4 4.1 fusion
  343.5 0.0 copy-done.4
  343.5 2.9 convolution_bitcast_fusion
  346.4 0.0 copy-start.5
  346.4 1.7 broadcast_in_dim.39
  348.2 2.0 gather_fusion
  350.2 5.5 fusion.2
  355.6 0.0 copy-done.5
  355.6 2.3 fusion.9
  358.0 2.4 broadcast_in_dim.37
  360.3 3.3 copy.15
  363.6 7.9 broadcast_in_dim.34
  371.4 20.5 %dynamic_update_slice.10 = f32[16,16,8,2048]{3,1,0,2:T(8,128)} dynamic-update-slice(f32[16,16,8,2048]{3,1,0,2:T(8,128)} %broadcast_in_dim.34, f32[16,1,8,2048]{3,1,0,2:T(1,128)} %copy.15, s32[]{:T(128)} %constant.42.clone.1, s32[]{:T(128)S(6)} %select_n.55, s32[]{:T(128)} %constant.42.clone.1, s32[]{:T(128)} %constant.42.clone.1) | dynamic-update-slice | bytes 2097156 | tf_op jit(solution)/shard_map/jit(dynamic_update_index_in_dim)/dynamic_update_slice | solution.py:54
  392.0 3.2 add_dynamic-update-slice_fusion
  395.2 15.5 %copy.17 = f32[16,16,8,2048]{3,2,1,0:T(8,128)S(1)} copy(f32[16,16,8,2048]{3,1,0,2:T(8,128)} %add_dynamic-update-slice_fusion) | data formatting | bytes 33554432 | tf_op jit(solution)/shard_map/add | solution.py:60
  410.7 20.1 %copy.32 = f32[2,8,128,2048]{3,1,2,0:T(8,128)} copy(f32[2,8,128,2048]{3,2,1,0:T(8,128)S(1)} %bitcast.82) | data formatting | bytes 33554432
  430.8 0.0 copy-start.1
  430.8 0.0 copy-start.2
  430.8 0.0 reduce-scatter.2.cloned.1.call-update
  430.8 0.0 copy-done
  430.8 0.8 copy-done.1
  431.6 0.4 fusion.38
  432.0 0.3 fusion.12
  432.2 649.9 %reduce-scatter.2.cloned.1.call-done = f32[16,2048]{1,0:T(8,128)} async-done(((f32[16,262144]{1,0:T(8,128)}), f32[16,2048]{1,0:T(8,128)}) %reduce-scatter.2.cloned.1.call-update) | async-done | bytes 131088 | tf_op jit(solution)/shard_map/reduce_scatter | solution.py:66
  1082.1 1.0 fusion.26
  1083.2 0.0 copy-start.3
  1083.2 12.9 %all-reduce.1 = (f32[16]{0:T(128)S(1)}, f32[16]{0:T(128)S(1)}) all-reduce(f32[16]{0:T(128)S(1)} %get-tuple-element.3, f32[16]{0:T(128)S(1)} %get-tuple-element.2), channel_id=1, replica_groups=mesh['row'=16,'col'=8] {'col'}, use_global_device_ids=true, to_apply=%region_2.3 | all-reduce | flops 32 | bytes 256 | tf_op jit(solution)/shard_map/psum | solution.py:81
  1096.0 52.3 %all-reduce = (f32[16]{0:T(128)S(1)}, f32[16]{0:T(128)S(1)}) all-reduce(f32[16]{0:T(128)S(1)} %get-tuple-element.6, f32[16]{0:T(128)S(1)} %get-tuple-element.7), channel_id=1, replica_groups=mesh['row'=16,'col'=8] {'row'}, use_global_device_ids=true, to_apply=%region_3.4 | all-reduce | flops 32 | bytes 256 | tf_op jit(solution)/shard_map/psum | solution.py:82
  1148.4 0.0 copy-done.2
  1148.4 0.4 fusion.13
  1148.8 0.7 copy.58
  1149.5 0.0 copy-done.3
  (4 shorter events, 0.0 us)
Async XLA Ops:
  7.2 423.6 %copy-start = (bf16[16,128,128]{2,1,0:T(8,128)(2,1)S(1)}, bf16[16,128,128]{2,1,0:T(8,128)(2,1)}, u32[]{:S(2)}) copy-start(bf16[16,128,128]{2,1,0:T(8,128)(2,1)} %param.12) | copy-start | bytes 1572868
  7.2 318.8 %all-gather.2.cloned.1.call-start = ((), (), s32[]{:S(2)}) async-start(), calls=%async_computation.1 | async-start | bytes 8454144 | tf_op jit(solution)/shard_map/all_gather | solution.py:20
  7.9 1074.2 %reduce-scatter.2.cloned.1.call-start = ((), (), s32[]{:S(2)}) async-start(), calls=%async_computation.2 | async-start | bytes 16908288 | tf_op jit(solution)/shard_map/reduce_scatter | solution.py:66
  336.6 6.9 copy-start.4
  346.4 9.2 copy-start.5
  430.8 0.8 copy-start.1
  430.8 717.6 %copy-start.2 = (bf16[16,128,128]{2,1,0:T(8,128)(2,1)S(1)}, bf16[16,128,128]{2,1,0:T(8,128)(2,1)}, u32[]{:S(2)}) copy-start(bf16[16,128,128]{2,1,0:T(8,128)(2,1)} %param.13) | copy-start | bytes 1572868
  1083.2 66.3 %copy-start.3 = (f32[16,2048]{1,0:T(8,128)}, f32[16,2048]{1,0:T(8,128)S(1)}, u32[]{:S(2)}) copy-start(f32[16,2048]{1,0:T(8,128)S(1)} %get-tuple-element.8) | copy-start | bytes 393220
Sparse Core Ops, SparseCore 0:
  9.7 316.1 all-gather.1
  430.9 651.1 reduce-scatter.1
